TPU v7x, 256 devices: a whole 4x4x8 slice. The times are simulated.
256 devices in a mesh: depth: 32 (over z, x), tile: 8 (over y, core).
Axes of the slice: x: 4, y: 4, z: 8, core: 2. Of those that a mesh axis runs over, the one named last changes fastest.
Arguments:
- tidal: float32 [32, 3, 131072], P('depth', None, 'tile'), may hold values from -1.5 to 1.5
- plane_weight: float32 [32], P('depth'), may hold values from 0.2 to 1
- plane_step: float32 [32], P('depth'), may hold values from 0.2 to 0.6
- ray_angle: float32 [131072], P('tile'), may hold values from -3.140625 to 3.140625
- dest_tile: int32 [32, 1024, 1], P('depth', 'tile'), may hold values from 0 to 7; in each aligned block of 128 rows (0 to 127, 128 to 255, ..., all dimensions but the last counted through in order) at most 32 rows name the same one
- dest_segment: int32 [32, 1024], P('depth', 'tile'), may hold values from 0 to 255
- interp: bfloat16 [32, 1024, 128, 128], P('depth', 'tile'), may hold values from -0.5 to 0.5
Outputs:
- potential_adjoint: float32 [32, 16, 16384], P('depth', 'tile')
Inputs may be any that keep to these rules, and one draw needn't show every extreme that they name: `dest_tile`: in each plane, the 128 blocks of one strip name no strip more than 32 times, a bound that some block reaches.
All inputs are finite; a program needn't handle non-finite values.
Results may differ from a plain program's by a relative error of at most 0.003.
Values sent between devices are 32-bit elements; how exact they have to be, the bound alone decides.
A program may use at most 64 MiB of HBM per device.

v0:
```python
import jax
import jax.numpy as jnp
from jax import lax
from jax.sharding import PartitionSpec as P

ROWS = 2
COLS = 16384


def from_behind(value, axis, steps):
    count = lax.axis_size(axis)
    leading, last = (max(0, -steps), min(count, count - steps))
    return lax.ppermute(value, axis, [(source, source + steps) for source in range(leading, last)])


def padded_2(shard, sides, width):
    for axis, dim in sides:
        count, length = (lax.axis_size(axis), shard.shape[dim])
        up = [(i, (i + 1) % count) for i in range(count - 1)]
        down = [(j, i) for i, j in up]
        last = lax.slice_in_dim(shard, length - width, length, axis=dim)
        leading = lax.slice_in_dim(shard, 0, width, axis=dim)
        before = lax.ppermute(last, axis, up)
        after = lax.ppermute(leading, axis, down)
        shard = jnp.concatenate([before, shard, after], axis=dim)
    return shard


def column_part(field):
    padded = jnp.pad(field, ((0, 0), (0, 0), (1, 1)))
    return 0.5 * (padded[:, :, :-2] - padded[:, :, 2:])


def smooth_cols(field):
    padded = jnp.pad(field, ((0, 0), (0, 0), (1, 1)))
    return 0.25 * padded[:, :, :-2] + 0.5 * field + 0.25 * padded[:, :, 2:]


def per_device(tidal, plane_weight, plane_step, ray_angle, dest_tile, dest_segment, interp):
    planes_here = tidal.shape[0]
    n_tile = lax.axis_size("tile")
    n_depth = lax.axis_size("depth")
    blocks_here = interp.shape[1]
    width = interp.shape[2]
    slots = 2 * blocks_here // n_tile
    segments = ROWS * COLS // width
    jxx = tidal[:, 0]
    jxy = tidal[:, 1]
    jyy = tidal[:, 2]
    local_terms = jnp.stack(
        [
            -jnp.sum(plane_weight[:, None] * (jxx - jyy) * 0.5, axis=0),
            -jnp.sum(plane_weight[:, None] * jxy, axis=0),
        ]
    )
    shear = lax.psum(local_terms, "depth")
    cross = -shear[0] * jnp.sin(2.0 * ray_angle) + shear[1] * jnp.cos(2.0 * ray_angle)
    seed_state = jnp.stack(
        [
            cross * jnp.cos(ray_angle),
            cross * jnp.sin(ray_angle),
            jnp.zeros_like(cross),
            jnp.zeros_like(cross),
        ]
    )

    def sweep(top):
        xb_one, xb_two, tb_one, tb_two = (top[0], top[1], top[2], top[3])
        step_len = plane_step[0]
        tp_one = tb_one + step_len * xb_one
        tp_two = tb_two + step_len * xb_two
        adjoints = [jnp.stack([-tp_one, -tp_two])]
        new_one = xb_one - (jxx[0] * tp_one + jxy[0] * tp_two)
        new_two = xb_two - (jxy[0] * tp_one + jyy[0] * tp_two)
        return (jnp.stack([new_one, new_two, tp_one, tp_two]), jnp.stack(adjoints[::-1]))

    is_last = lax.axis_index("depth") == n_depth - 1

    def relay_step(turn, top):
        bottom, unused = sweep(top)
        incoming = from_behind(bottom, "depth", -1)
        return jnp.where(is_last, seed_state, incoming)

    top_state = lax.fori_loop(0, n_depth - 1, relay_step, seed_state)
    unused_state, deflection_bar = sweep(top_state)
    abar = deflection_bar.astype(jnp.bfloat16).reshape(planes_here, 2, blocks_here, width)
    contrib = jnp.einsum("pcbr,pbrk->pbck", abar, interp, preferred_element_type=jnp.float32)
    dest = dest_tile[:, :, 0]
    order_mask = jnp.arange(blocks_here)[None, :] < jnp.arange(blocks_here)[:, None]
    same_dest = dest[:, :, None] == dest[:, None, :]
    rank = jnp.sum(jnp.logical_and(same_dest, order_mask[None]), axis=2)
    slot = dest[0] * slots + rank[0]
    send_data = jnp.zeros((n_tile * slots, 2, width), jnp.float32).at[slot].set(contrib[0])
    send_ids = jnp.zeros((n_tile * slots,), jnp.int32).at[slot].set(dest_segment[0])
    got_data = lax.all_to_all(
        send_data.reshape(n_tile, slots, 2, width), "tile", split_axis=0, concat_axis=0, tiled=True
    )
    got_ids = lax.all_to_all(
        send_ids.reshape(n_tile, slots), "tile", split_axis=0, concat_axis=0, tiled=True
    )
    summed = (
        jnp.zeros((segments, 2, width), jnp.float32)
        .at[got_ids.reshape(-1)]
        .add(got_data.reshape(-1, 2, width))
    )
    plane_maps = [jnp.transpose(summed, (1, 0, 2)).reshape(2, ROWS, COLS)]
    maps = jnp.stack(plane_maps)
    ay_ext = padded_2(maps[:, 1], (("tile", 1),), 1)
    raw = column_part(maps[:, 0]) + 0.5 * (ay_ext[:, :-2, :] - ay_ext[:, 2:, :])
    raw_ext = padded_2(raw, (("tile", 1),), 1)
    rows_done = 0.25 * raw_ext[:, :-2, :] + 0.5 * raw_ext[:, 1:-1, :] + 0.25 * raw_ext[:, 2:, :]
    return smooth_cols(rows_done)


def solution(mesh):
    return jax.shard_map(
        per_device,
        mesh=mesh,
        in_specs=(
            P("depth", None, "tile"),
            P("depth"),
            P("depth"),
            P("tile"),
            P("depth", "tile", None),
            P("depth", "tile"),
            P("depth", "tile", None, None),
        ),
        out_specs=P("depth", "tile", None),
        check_vma=False,
    )
```

profile of v0, /device:TPU:103, one launch (start us, length us, event | category | flops | bytes accessed | tf_op | source)
XLA Modules:
  0.0 640.3 jit_solution(10379709504389961642)
XLA Ops:
  19.2 129.9 %all-reduce.4.cloned.1.call-done = f32[2,16384]{1,0:T(2,128)} async-done(((f32[2,16384]{1,0:T(2,128)}), f32[2,16384]{1,0:T(2,128)}) %all-reduce.4.cloned.1.call-update) | async-done | bytes 131088 | tf_op jit(solution)/shard_map/psum | solution.py:56
  151.7 387.7 %while.10 = (s32[]{:T(128)}, f32[4,16384]{1,0:T(4,128)S(1)}, pred[]{:T(512)}, f32[1,1,16384]{2,1,0:T(1,128)S(1)}, f32[1]{0:T(128)}, /*index=5*/f32[1,1,16384]{2,...) while((s32[]{:T(128)}, f32[4,16384]{1,0:T(4,128)S(1)}, pred[]{:T(512)}, ...), condition=%wide.region_4.5_spmd, body=%wide.region_3.4_spmd.sunk | while | flops 458754 | bytes 3342474 | solution.py:84
  166.8 8.5 %collective-permute-done = f32[4,16384]{1,0:T(4,128)S(1)} collective-permute-done((f32[4,16384]{1,0:T(4,128)S(1)}, f32[4,16384]{1,0:T(4,128)S(1)}, u32[]{:S(2)}, u32[]{:S(2)}) %collective-permute-start) | collective-permute-done | bytes 262176 | tf_op jit(solution)/shard_map/while/body/eval_jaxpr/ppermute | solution.py:13
  178.7 8.5 %collective-permute-done = f32[4,16384]{1,0:T(4,128)S(1)} collective-permute-done((f32[4,16384]{1,0:T(4,128)S(1)}, f32[4,16384]{1,0:T(4,128)S(1)}, u32[]{:S(2)}, u32[]{:S(2)}) %collective-permute-start) | collective-permute-done | bytes 262176 | tf_op jit(solution)/shard_map/while/body/eval_jaxpr/ppermute | solution.py:13
  190.5 8.5 %collective-permute-done = f32[4,16384]{1,0:T(4,128)S(1)} collective-permute-done((f32[4,16384]{1,0:T(4,128)S(1)}, f32[4,16384]{1,0:T(4,128)S(1)}, u32[]{:S(2)}, u32[]{:S(2)}) %collective-permute-start) | collective-permute-done | bytes 262176 | tf_op jit(solution)/shard_map/while/body/eval_jaxpr/ppermute | solution.py:13
  202.4 8.7 %collective-permute-done = f32[4,16384]{1,0:T(4,128)S(1)} collective-permute-done((f32[4,16384]{1,0:T(4,128)S(1)}, f32[4,16384]{1,0:T(4,128)S(1)}, u32[]{:S(2)}, u32[]{:S(2)}) %collective-permute-start) | collective-permute-done | bytes 262176 | tf_op jit(solution)/shard_map/while/body/eval_jaxpr/ppermute | solution.py:13
  214.5 9.9 %collective-permute-done = f32[4,16384]{1,0:T(4,128)S(1)} collective-permute-done((f32[4,16384]{1,0:T(4,128)S(1)}, f32[4,16384]{1,0:T(4,128)S(1)}, u32[]{:S(2)}, u32[]{:S(2)}) %collective-permute-start) | collective-permute-done | bytes 262176 | tf_op jit(solution)/shard_map/while/body/eval_jaxpr/ppermute | solution.py:13
  227.7 11.0 %collective-permute-done = f32[4,16384]{1,0:T(4,128)S(1)} collective-permute-done((f32[4,16384]{1,0:T(4,128)S(1)}, f32[4,16384]{1,0:T(4,128)S(1)}, u32[]{:S(2)}, u32[]{:S(2)}) %collective-permute-start) | collective-permute-done | bytes 262176 | tf_op jit(solution)/shard_map/while/body/eval_jaxpr/ppermute | solution.py:13
  242.0 10.8 %collective-permute-done = f32[4,16384]{1,0:T(4,128)S(1)} collective-permute-done((f32[4,16384]{1,0:T(4,128)S(1)}, f32[4,16384]{1,0:T(4,128)S(1)}, u32[]{:S(2)}, u32[]{:S(2)}) %collective-permute-start) | collective-permute-done | bytes 262176 | tf_op jit(solution)/shard_map/while/body/eval_jaxpr/ppermute | solution.py:13
  256.1 9.9 %collective-permute-done = f32[4,16384]{1,0:T(4,128)S(1)} collective-permute-done((f32[4,16384]{1,0:T(4,128)S(1)}, f32[4,16384]{1,0:T(4,128)S(1)}, u32[]{:S(2)}, u32[]{:S(2)}) %collective-permute-start) | collective-permute-done | bytes 262176 | tf_op jit(solution)/shard_map/while/body/eval_jaxpr/ppermute | solution.py:13
  269.4 9.1 %collective-permute-done = f32[4,16384]{1,0:T(4,128)S(1)} collective-permute-done((f32[4,16384]{1,0:T(4,128)S(1)}, f32[4,16384]{1,0:T(4,128)S(1)}, u32[]{:S(2)}, u32[]{:S(2)}) %collective-permute-start) | collective-permute-done | bytes 262176 | tf_op jit(solution)/shard_map/while/body/eval_jaxpr/ppermute | solution.py:13
  281.8 8.5 %collective-permute-done = f32[4,16384]{1,0:T(4,128)S(1)} collective-permute-done((f32[4,16384]{1,0:T(4,128)S(1)}, f32[4,16384]{1,0:T(4,128)S(1)}, u32[]{:S(2)}, u32[]{:S(2)}) %collective-permute-start) | collective-permute-done | bytes 262176 | tf_op jit(solution)/shard_map/while/body/eval_jaxpr/ppermute | solution.py:13
  293.7 8.5 %collective-permute-done = f32[4,16384]{1,0:T(4,128)S(1)} collective-permute-done((f32[4,16384]{1,0:T(4,128)S(1)}, f32[4,16384]{1,0:T(4,128)S(1)}, u32[]{:S(2)}, u32[]{:S(2)}) %collective-permute-start) | collective-permute-done | bytes 262176 | tf_op jit(solution)/shard_map/while/body/eval_jaxpr/ppermute | solution.py:13
  317.4 8.5 %collective-permute-done = f32[4,16384]{1,0:T(4,128)S(1)} collective-permute-done((f32[4,16384]{1,0:T(4,128)S(1)}, f32[4,16384]{1,0:T(4,128)S(1)}, u32[]{:S(2)}, u32[]{:S(2)}) %collective-permute-start) | collective-permute-done | bytes 262176 | tf_op jit(solution)/shard_map/while/body/eval_jaxpr/ppermute | solution.py:13
  329.3 8.5 %collective-permute-done = f32[4,16384]{1,0:T(4,128)S(1)} collective-permute-done((f32[4,16384]{1,0:T(4,128)S(1)}, f32[4,16384]{1,0:T(4,128)S(1)}, u32[]{:S(2)}, u32[]{:S(2)}) %collective-permute-start) | collective-permute-done | bytes 262176 | tf_op jit(solution)/shard_map/while/body/eval_jaxpr/ppermute | solution.py:13
  341.1 8.5 %collective-permute-done = f32[4,16384]{1,0:T(4,128)S(1)} collective-permute-done((f32[4,16384]{1,0:T(4,128)S(1)}, f32[4,16384]{1,0:T(4,128)S(1)}, u32[]{:S(2)}, u32[]{:S(2)}) %collective-permute-start) | collective-permute-done | bytes 262176 | tf_op jit(solution)/shard_map/while/body/eval_jaxpr/ppermute | solution.py:13
  353.0 8.6 %collective-permute-done = f32[4,16384]{1,0:T(4,128)S(1)} collective-permute-done((f32[4,16384]{1,0:T(4,128)S(1)}, f32[4,16384]{1,0:T(4,128)S(1)}, u32[]{:S(2)}, u32[]{:S(2)}) %collective-permute-start) | collective-permute-done | bytes 262176 | tf_op jit(solution)/shard_map/while/body/eval_jaxpr/ppermute | solution.py:13
  365.0 9.8 %collective-permute-done = f32[4,16384]{1,0:T(4,128)S(1)} collective-permute-done((f32[4,16384]{1,0:T(4,128)S(1)}, f32[4,16384]{1,0:T(4,128)S(1)}, u32[]{:S(2)}, u32[]{:S(2)}) %collective-permute-start) | collective-permute-done | bytes 262176 | tf_op jit(solution)/shard_map/while/body/eval_jaxpr/ppermute | solution.py:13
  378.1 10.9 %collective-permute-done = f32[4,16384]{1,0:T(4,128)S(1)} collective-permute-done((f32[4,16384]{1,0:T(4,128)S(1)}, f32[4,16384]{1,0:T(4,128)S(1)}, u32[]{:S(2)}, u32[]{:S(2)}) %collective-permute-start) | collective-permute-done | bytes 262176 | tf_op jit(solution)/shard_map/while/body/eval_jaxpr/ppermute | solution.py:13
  392.3 10.9 %collective-permute-done = f32[4,16384]{1,0:T(4,128)S(1)} collective-permute-done((f32[4,16384]{1,0:T(4,128)S(1)}, f32[4,16384]{1,0:T(4,128)S(1)}, u32[]{:S(2)}, u32[]{:S(2)}) %collective-permute-start) | collective-permute-done | bytes 262176 | tf_op jit(solution)/shard_map/while/body/eval_jaxpr/ppermute | solution.py:13
  406.6 10.0 %collective-permute-done = f32[4,16384]{1,0:T(4,128)S(1)} collective-permute-done((f32[4,16384]{1,0:T(4,128)S(1)}, f32[4,16384]{1,0:T(4,128)S(1)}, u32[]{:S(2)}, u32[]{:S(2)}) %collective-permute-start) | collective-permute-done | bytes 262176 | tf_op jit(solution)/shard_map/while/body/eval_jaxpr/ppermute | solution.py:13
  419.9 9.2 %collective-permute-done = f32[4,16384]{1,0:T(4,128)S(1)} collective-permute-done((f32[4,16384]{1,0:T(4,128)S(1)}, f32[4,16384]{1,0:T(4,128)S(1)}, u32[]{:S(2)}, u32[]{:S(2)}) %collective-permute-start) | collective-permute-done | bytes 262176 | tf_op jit(solution)/shard_map/while/body/eval_jaxpr/ppermute | solution.py:13
  432.5 8.5 %collective-permute-done = f32[4,16384]{1,0:T(4,128)S(1)} collective-permute-done((f32[4,16384]{1,0:T(4,128)S(1)}, f32[4,16384]{1,0:T(4,128)S(1)}, u32[]{:S(2)}, u32[]{:S(2)}) %collective-permute-start) | collective-permute-done | bytes 262176 | tf_op jit(solution)/shard_map/while/body/eval_jaxpr/ppermute | solution.py:13
  444.3 8.5 %collective-permute-done = f32[4,16384]{1,0:T(4,128)S(1)} collective-permute-done((f32[4,16384]{1,0:T(4,128)S(1)}, f32[4,16384]{1,0:T(4,128)S(1)}, u32[]{:S(2)}, u32[]{:S(2)}) %collective-permute-start) | collective-permute-done | bytes 262176 | tf_op jit(solution)/shard_map/while/body/eval_jaxpr/ppermute | solution.py:13
  456.2 8.5 %collective-permute-done = f32[4,16384]{1,0:T(4,128)S(1)} collective-permute-done((f32[4,16384]{1,0:T(4,128)S(1)}, f32[4,16384]{1,0:T(4,128)S(1)}, u32[]{:S(2)}, u32[]{:S(2)}) %collective-permute-start) | collective-permute-done | bytes 262176 | tf_op jit(solution)/shard_map/while/body/eval_jaxpr/ppermute | solution.py:13
  479.9 8.5 %collective-permute-done = f32[4,16384]{1,0:T(4,128)S(1)} collective-permute-done((f32[4,16384]{1,0:T(4,128)S(1)}, f32[4,16384]{1,0:T(4,128)S(1)}, u32[]{:S(2)}, u32[]{:S(2)}) %collective-permute-start) | collective-permute-done | bytes 262176 | tf_op jit(solution)/shard_map/while/body/eval_jaxpr/ppermute | solution.py:13
  491.8 8.5 %collective-permute-done = f32[4,16384]{1,0:T(4,128)S(1)} collective-permute-done((f32[4,16384]{1,0:T(4,128)S(1)}, f32[4,16384]{1,0:T(4,128)S(1)}, u32[]{:S(2)}, u32[]{:S(2)}) %collective-permute-start) | collective-permute-done | bytes 262176 | tf_op jit(solution)/shard_map/while/body/eval_jaxpr/ppermute | solution.py:13
  515.5 9.6 %collective-permute-done = f32[4,16384]{1,0:T(4,128)S(1)} collective-permute-done((f32[4,16384]{1,0:T(4,128)S(1)}, f32[4,16384]{1,0:T(4,128)S(1)}, u32[]{:S(2)}, u32[]{:S(2)}) %collective-permute-start) | collective-permute-done | bytes 262176 | tf_op jit(solution)/shard_map/while/body/eval_jaxpr/ppermute | solution.py:13
  528.5 10.8 %collective-permute-done = f32[4,16384]{1,0:T(4,128)S(1)} collective-permute-done((f32[4,16384]{1,0:T(4,128)S(1)}, f32[4,16384]{1,0:T(4,128)S(1)}, u32[]{:S(2)}, u32[]{:S(2)}) %collective-permute-start) | collective-permute-done | bytes 262176 | tf_op jit(solution)/shard_map/while/body/eval_jaxpr/ppermute | solution.py:13
  543.8 12.5 %scatter_fusion = f32[256,2,128]{2,1,0:T(2,128)} fusion(f32[256,2,128]{2,1,0:T(2,128)} %broadcast.154.clone, s32[128]{0:T(128)S(1)} %fusion.14, f32[128,2,128]{2,1,0:T(2,128)S(1)} %fusion.4), kind=kCustom, calls=%fused_computation.1 | custom fusion | bytes 393728 | tf_op jit(solution)/shard_map/scatter | solution.py:93
  556.2 43.4 %all-to-all-start.1 = ((f32[8,32,2,128]{3,2,1,0:T(2,128)}), f32[8,32,2,128]{3,2,1,0:T(2,128)S(1)}, u32[]{:S(2)}, u32[]{:S(2)}) async-start(f32[8,32,2,128]{3,2,1,0:T(2,128)} %bitcast.21), calls=%async_computation.1 | async-start | bytes 524288 | tf_op jit(solution)/shard_map/all_to_all | solution.py:95
  606.2 8.7 %scatter_fusion.1 = f32[256,2,128]{2,1,0:T(2,128)S(1)} fusion(f32[256,2,128]{2,1,0:T(2,128)S(1)} %broadcast.154, s32[256]{0:T(256)S(1)} %bitcast.85, f32[256,2,128]{2,1,0:T(2,128)S(1)} %bitcast.80), kind=kCustom, calls=%fused_computation.2 | custom fusion | flops 65536 | bytes 787456 | tf_op jit(solution)/shard_map/scatter-add | solution.py:104
  (201 shorter events, 179.8 us)
Async XLA Ops:
  6.5 142.5 %all-reduce.4.cloned.1.call-start = ((), (), s32[]{:S(2)}) async-start(), calls=%async_computation.2 | async-start | bytes 262144 | tf_op jit(solution)/shard_map/psum | solution.py:56
  12.4 543.8 %all-to-all-start = ((s32[8,1,32]{2,1,0:T(1,128)}), s32[8,1,32]{2,1,0:T(1,128)S(1)}, u32[]{:S(2)}, u32[]{:S(2)}) async-start(s32[8,1,32]{2,1,0:T(1,128)} %all_to_all.9), calls=%async_computation | async-start | bytes 8192 | tf_op jit(solution)/shard_map/all_to_all | solution.py:98
  153.0 10.4 %collective-permute-start = (f32[4,16384]{1,0:T(4,128)S(1)}, f32[4,16384]{1,0:T(4,128)S(1)}, u32[]{:S(2)}, u32[]{:S(2)}) collective-permute-start(f32[4,16384]{1,0:T(4,128)S(1)} %pad_maximum_fusion.7), channel_id=1, source_target_pairs={{8,0},{16,8},{24,16},{32,24},{40,32},{48,40},{56,48},{64,56},{72,6... | collective-permute-start | bytes 786440 | tf_op jit(solution)/shard_map/while/body/eval_jaxpr/ppermute | solution.py:13
  164.9 10.4 %collective-permute-start = (f32[4,16384]{1,0:T(4,128)S(1)}, f32[4,16384]{1,0:T(4,128)S(1)}, u32[]{:S(2)}, u32[]{:S(2)}) collective-permute-start(f32[4,16384]{1,0:T(4,128)S(1)} %pad_maximum_fusion.7), channel_id=1, source_target_pairs={{8,0},{16,8},{24,16},{32,24},{40,32},{48,40},{56,48},{64,56},{72,6... | collective-permute-start | bytes 786440 | tf_op jit(solution)/shard_map/while/body/eval_jaxpr/ppermute | solution.py:13
  176.7 10.4 %collective-permute-start = (f32[4,16384]{1,0:T(4,128)S(1)}, f32[4,16384]{1,0:T(4,128)S(1)}, u32[]{:S(2)}, u32[]{:S(2)}) collective-permute-start(f32[4,16384]{1,0:T(4,128)S(1)} %pad_maximum_fusion.7), channel_id=1, source_target_pairs={{8,0},{16,8},{24,16},{32,24},{40,32},{48,40},{56,48},{64,56},{72,6... | collective-permute-start | bytes 786440 | tf_op jit(solution)/shard_map/while/body/eval_jaxpr/ppermute | solution.py:13
  188.6 10.4 %collective-permute-start = (f32[4,16384]{1,0:T(4,128)S(1)}, f32[4,16384]{1,0:T(4,128)S(1)}, u32[]{:S(2)}, u32[]{:S(2)}) collective-permute-start(f32[4,16384]{1,0:T(4,128)S(1)} %pad_maximum_fusion.7), channel_id=1, source_target_pairs={{8,0},{16,8},{24,16},{32,24},{40,32},{48,40},{56,48},{64,56},{72,6... | collective-permute-start | bytes 786440 | tf_op jit(solution)/shard_map/while/body/eval_jaxpr/ppermute | solution.py:13
  200.5 10.6 %collective-permute-start = (f32[4,16384]{1,0:T(4,128)S(1)}, f32[4,16384]{1,0:T(4,128)S(1)}, u32[]{:S(2)}, u32[]{:S(2)}) collective-permute-start(f32[4,16384]{1,0:T(4,128)S(1)} %pad_maximum_fusion.7), channel_id=1, source_target_pairs={{8,0},{16,8},{24,16},{32,24},{40,32},{48,40},{56,48},{64,56},{72,6... | collective-permute-start | bytes 786440 | tf_op jit(solution)/shard_map/while/body/eval_jaxpr/ppermute | solution.py:13
  212.5 11.8 %collective-permute-start = (f32[4,16384]{1,0:T(4,128)S(1)}, f32[4,16384]{1,0:T(4,128)S(1)}, u32[]{:S(2)}, u32[]{:S(2)}) collective-permute-start(f32[4,16384]{1,0:T(4,128)S(1)} %pad_maximum_fusion.7), channel_id=1, source_target_pairs={{8,0},{16,8},{24,16},{32,24},{40,32},{48,40},{56,48},{64,56},{72,6... | collective-permute-start | bytes 786440 | tf_op jit(solution)/shard_map/while/body/eval_jaxpr/ppermute | solution.py:13
  225.7 12.9 %collective-permute-start = (f32[4,16384]{1,0:T(4,128)S(1)}, f32[4,16384]{1,0:T(4,128)S(1)}, u32[]{:S(2)}, u32[]{:S(2)}) collective-permute-start(f32[4,16384]{1,0:T(4,128)S(1)} %pad_maximum_fusion.7), channel_id=1, source_target_pairs={{8,0},{16,8},{24,16},{32,24},{40,32},{48,40},{56,48},{64,56},{72,6... | collective-permute-start | bytes 786440 | tf_op jit(solution)/shard_map/while/body/eval_jaxpr/ppermute | solution.py:13
  240.1 12.7 %collective-permute-start = (f32[4,16384]{1,0:T(4,128)S(1)}, f32[4,16384]{1,0:T(4,128)S(1)}, u32[]{:S(2)}, u32[]{:S(2)}) collective-permute-start(f32[4,16384]{1,0:T(4,128)S(1)} %pad_maximum_fusion.7), channel_id=1, source_target_pairs={{8,0},{16,8},{24,16},{32,24},{40,32},{48,40},{56,48},{64,56},{72,6... | collective-permute-start | bytes 786440 | tf_op jit(solution)/shard_map/while/body/eval_jaxpr/ppermute | solution.py:13
  254.2 11.9 %collective-permute-start = (f32[4,16384]{1,0:T(4,128)S(1)}, f32[4,16384]{1,0:T(4,128)S(1)}, u32[]{:S(2)}, u32[]{:S(2)}) collective-permute-start(f32[4,16384]{1,0:T(4,128)S(1)} %pad_maximum_fusion.7), channel_id=1, source_target_pairs={{8,0},{16,8},{24,16},{32,24},{40,32},{48,40},{56,48},{64,56},{72,6... | collective-permute-start | bytes 786440 | tf_op jit(solution)/shard_map/while/body/eval_jaxpr/ppermute | solution.py:13
  267.5 11.0 %collective-permute-start = (f32[4,16384]{1,0:T(4,128)S(1)}, f32[4,16384]{1,0:T(4,128)S(1)}, u32[]{:S(2)}, u32[]{:S(2)}) collective-permute-start(f32[4,16384]{1,0:T(4,128)S(1)} %pad_maximum_fusion.7), channel_id=1, source_target_pairs={{8,0},{16,8},{24,16},{32,24},{40,32},{48,40},{56,48},{64,56},{72,6... | collective-permute-start | bytes 786440 | tf_op jit(solution)/shard_map/while/body/eval_jaxpr/ppermute | solution.py:13
  279.9 10.4 %collective-permute-start = (f32[4,16384]{1,0:T(4,128)S(1)}, f32[4,16384]{1,0:T(4,128)S(1)}, u32[]{:S(2)}, u32[]{:S(2)}) collective-permute-start(f32[4,16384]{1,0:T(4,128)S(1)} %pad_maximum_fusion.7), channel_id=1, source_target_pairs={{8,0},{16,8},{24,16},{32,24},{40,32},{48,40},{56,48},{64,56},{72,6... | collective-permute-start | bytes 786440 | tf_op jit(solution)/shard_map/while/body/eval_jaxpr/ppermute | solution.py:13
  291.8 10.4 %collective-permute-start = (f32[4,16384]{1,0:T(4,128)S(1)}, f32[4,16384]{1,0:T(4,128)S(1)}, u32[]{:S(2)}, u32[]{:S(2)}) collective-permute-start(f32[4,16384]{1,0:T(4,128)S(1)} %pad_maximum_fusion.7), channel_id=1, source_target_pairs={{8,0},{16,8},{24,16},{32,24},{40,32},{48,40},{56,48},{64,56},{72,6... | collective-permute-start | bytes 786440 | tf_op jit(solution)/shard_map/while/body/eval_jaxpr/ppermute | solution.py:13
  303.6 10.4 %collective-permute-start = (f32[4,16384]{1,0:T(4,128)S(1)}, f32[4,16384]{1,0:T(4,128)S(1)}, u32[]{:S(2)}, u32[]{:S(2)}) collective-permute-start(f32[4,16384]{1,0:T(4,128)S(1)} %pad_maximum_fusion.7), channel_id=1, source_target_pairs={{8,0},{16,8},{24,16},{32,24},{40,32},{48,40},{56,48},{64,56},{72,6... | collective-permute-start | bytes 786440 | tf_op jit(solution)/shard_map/while/body/eval_jaxpr/ppermute | solution.py:13
  315.5 10.4 %collective-permute-start = (f32[4,16384]{1,0:T(4,128)S(1)}, f32[4,16384]{1,0:T(4,128)S(1)}, u32[]{:S(2)}, u32[]{:S(2)}) collective-permute-start(f32[4,16384]{1,0:T(4,128)S(1)} %pad_maximum_fusion.7), channel_id=1, source_target_pairs={{8,0},{16,8},{24,16},{32,24},{40,32},{48,40},{56,48},{64,56},{72,6... | collective-permute-start | bytes 786440 | tf_op jit(solution)/shard_map/while/body/eval_jaxpr/ppermute | solution.py:13
  327.4 10.4 %collective-permute-start = (f32[4,16384]{1,0:T(4,128)S(1)}, f32[4,16384]{1,0:T(4,128)S(1)}, u32[]{:S(2)}, u32[]{:S(2)}) collective-permute-start(f32[4,16384]{1,0:T(4,128)S(1)} %pad_maximum_fusion.7), channel_id=1, source_target_pairs={{8,0},{16,8},{24,16},{32,24},{40,32},{48,40},{56,48},{64,56},{72,6... | collective-permute-start | bytes 786440 | tf_op jit(solution)/shard_map/while/body/eval_jaxpr/ppermute | solution.py:13
  339.2 10.4 %collective-permute-start = (f32[4,16384]{1,0:T(4,128)S(1)}, f32[4,16384]{1,0:T(4,128)S(1)}, u32[]{:S(2)}, u32[]{:S(2)}) collective-permute-start(f32[4,16384]{1,0:T(4,128)S(1)} %pad_maximum_fusion.7), channel_id=1, source_target_pairs={{8,0},{16,8},{24,16},{32,24},{40,32},{48,40},{56,48},{64,56},{72,6... | collective-permute-start | bytes 786440 | tf_op jit(solution)/shard_map/while/body/eval_jaxpr/ppermute | solution.py:13
  351.1 10.5 %collective-permute-start = (f32[4,16384]{1,0:T(4,128)S(1)}, f32[4,16384]{1,0:T(4,128)S(1)}, u32[]{:S(2)}, u32[]{:S(2)}) collective-permute-start(f32[4,16384]{1,0:T(4,128)S(1)} %pad_maximum_fusion.7), channel_id=1, source_target_pairs={{8,0},{16,8},{24,16},{32,24},{40,32},{48,40},{56,48},{64,56},{72,6... | collective-permute-start | bytes 786440 | tf_op jit(solution)/shard_map/while/body/eval_jaxpr/ppermute | solution.py:13
  363.0 11.7 %collective-permute-start = (f32[4,16384]{1,0:T(4,128)S(1)}, f32[4,16384]{1,0:T(4,128)S(1)}, u32[]{:S(2)}, u32[]{:S(2)}) collective-permute-start(f32[4,16384]{1,0:T(4,128)S(1)} %pad_maximum_fusion.7), channel_id=1, source_target_pairs={{8,0},{16,8},{24,16},{32,24},{40,32},{48,40},{56,48},{64,56},{72,6... | collective-permute-start | bytes 786440 | tf_op jit(solution)/shard_map/while/body/eval_jaxpr/ppermute | solution.py:13
  376.1 12.8 %collective-permute-start = (f32[4,16384]{1,0:T(4,128)S(1)}, f32[4,16384]{1,0:T(4,128)S(1)}, u32[]{:S(2)}, u32[]{:S(2)}) collective-permute-start(f32[4,16384]{1,0:T(4,128)S(1)} %pad_maximum_fusion.7), channel_id=1, source_target_pairs={{8,0},{16,8},{24,16},{32,24},{40,32},{48,40},{56,48},{64,56},{72,6... | collective-permute-start | bytes 786440 | tf_op jit(solution)/shard_map/while/body/eval_jaxpr/ppermute | solution.py:13
  390.4 12.8 %collective-permute-start = (f32[4,16384]{1,0:T(4,128)S(1)}, f32[4,16384]{1,0:T(4,128)S(1)}, u32[]{:S(2)}, u32[]{:S(2)}) collective-permute-start(f32[4,16384]{1,0:T(4,128)S(1)} %pad_maximum_fusion.7), channel_id=1, source_target_pairs={{8,0},{16,8},{24,16},{32,24},{40,32},{48,40},{56,48},{64,56},{72,6... | collective-permute-start | bytes 786440 | tf_op jit(solution)/shard_map/while/body/eval_jaxpr/ppermute | solution.py:13
  404.6 12.0 %collective-permute-start = (f32[4,16384]{1,0:T(4,128)S(1)}, f32[4,16384]{1,0:T(4,128)S(1)}, u32[]{:S(2)}, u32[]{:S(2)}) collective-permute-start(f32[4,16384]{1,0:T(4,128)S(1)} %pad_maximum_fusion.7), channel_id=1, source_target_pairs={{8,0},{16,8},{24,16},{32,24},{40,32},{48,40},{56,48},{64,56},{72,6... | collective-permute-start | bytes 786440 | tf_op jit(solution)/shard_map/while/body/eval_jaxpr/ppermute | solution.py:13
  418.0 11.1 %collective-permute-start = (f32[4,16384]{1,0:T(4,128)S(1)}, f32[4,16384]{1,0:T(4,128)S(1)}, u32[]{:S(2)}, u32[]{:S(2)}) collective-permute-start(f32[4,16384]{1,0:T(4,128)S(1)} %pad_maximum_fusion.7), channel_id=1, source_target_pairs={{8,0},{16,8},{24,16},{32,24},{40,32},{48,40},{56,48},{64,56},{72,6... | collective-permute-start | bytes 786440 | tf_op jit(solution)/shard_map/while/body/eval_jaxpr/ppermute | solution.py:13
  430.5 10.4 %collective-permute-start = (f32[4,16384]{1,0:T(4,128)S(1)}, f32[4,16384]{1,0:T(4,128)S(1)}, u32[]{:S(2)}, u32[]{:S(2)}) collective-permute-start(f32[4,16384]{1,0:T(4,128)S(1)} %pad_maximum_fusion.7), channel_id=1, source_target_pairs={{8,0},{16,8},{24,16},{32,24},{40,32},{48,40},{56,48},{64,56},{72,6... | collective-permute-start | bytes 786440 | tf_op jit(solution)/shard_map/while/body/eval_jaxpr/ppermute | solution.py:13
  442.4 10.4 %collective-permute-start = (f32[4,16384]{1,0:T(4,128)S(1)}, f32[4,16384]{1,0:T(4,128)S(1)}, u32[]{:S(2)}, u32[]{:S(2)}) collective-permute-start(f32[4,16384]{1,0:T(4,128)S(1)} %pad_maximum_fusion.7), channel_id=1, source_target_pairs={{8,0},{16,8},{24,16},{32,24},{40,32},{48,40},{56,48},{64,56},{72,6... | collective-permute-start | bytes 786440 | tf_op jit(solution)/shard_map/while/body/eval_jaxpr/ppermute | solution.py:13
  454.3 10.4 %collective-permute-start = (f32[4,16384]{1,0:T(4,128)S(1)}, f32[4,16384]{1,0:T(4,128)S(1)}, u32[]{:S(2)}, u32[]{:S(2)}) collective-permute-start(f32[4,16384]{1,0:T(4,128)S(1)} %pad_maximum_fusion.7), channel_id=1, source_target_pairs={{8,0},{16,8},{24,16},{32,24},{40,32},{48,40},{56,48},{64,56},{72,6... | collective-permute-start | bytes 786440 | tf_op jit(solution)/shard_map/while/body/eval_jaxpr/ppermute | solution.py:13
  478.0 10.4 %collective-permute-start = (f32[4,16384]{1,0:T(4,128)S(1)}, f32[4,16384]{1,0:T(4,128)S(1)}, u32[]{:S(2)}, u32[]{:S(2)}) collective-permute-start(f32[4,16384]{1,0:T(4,128)S(1)} %pad_maximum_fusion.7), channel_id=1, source_target_pairs={{8,0},{16,8},{24,16},{32,24},{40,32},{48,40},{56,48},{64,56},{72,6... | collective-permute-start | bytes 786440 | tf_op jit(solution)/shard_map/while/body/eval_jaxpr/ppermute | solution.py:13
  489.8 10.4 %collective-permute-start = (f32[4,16384]{1,0:T(4,128)S(1)}, f32[4,16384]{1,0:T(4,128)S(1)}, u32[]{:S(2)}, u32[]{:S(2)}) collective-permute-start(f32[4,16384]{1,0:T(4,128)S(1)} %pad_maximum_fusion.7), channel_id=1, source_target_pairs={{8,0},{16,8},{24,16},{32,24},{40,32},{48,40},{56,48},{64,56},{72,6... | collective-permute-start | bytes 786440 | tf_op jit(solution)/shard_map/while/body/eval_jaxpr/ppermute | solution.py:13
  513.6 11.6 %collective-permute-start = (f32[4,16384]{1,0:T(4,128)S(1)}, f32[4,16384]{1,0:T(4,128)S(1)}, u32[]{:S(2)}, u32[]{:S(2)}) collective-permute-start(f32[4,16384]{1,0:T(4,128)S(1)} %pad_maximum_fusion.7), channel_id=1, source_target_pairs={{8,0},{16,8},{24,16},{32,24},{40,32},{48,40},{56,48},{64,56},{72,6... | collective-permute-start | bytes 786440 | tf_op jit(solution)/shard_map/while/body/eval_jaxpr/ppermute | solution.py:13
  526.6 12.7 %collective-permute-start = (f32[4,16384]{1,0:T(4,128)S(1)}, f32[4,16384]{1,0:T(4,128)S(1)}, u32[]{:S(2)}, u32[]{:S(2)}) collective-permute-start(f32[4,16384]{1,0:T(4,128)S(1)} %pad_maximum_fusion.7), channel_id=1, source_target_pairs={{8,0},{16,8},{24,16},{32,24},{40,32},{48,40},{56,48},{64,56},{72,6... | collective-permute-start | bytes 786440 | tf_op jit(solution)/shard_map/while/body/eval_jaxpr/ppermute | solution.py:13
  556.2 49.9 %all-to-all-start.1 = ((f32[8,32,2,128]{3,2,1,0:T(2,128)}), f32[8,32,2,128]{3,2,1,0:T(2,128)S(1)}, u32[]{:S(2)}, u32[]{:S(2)}) async-start(f32[8,32,2,128]{3,2,1,0:T(2,128)} %bitcast.21), calls=%async_computation.1 | async-start | bytes 524288 | tf_op jit(solution)/shard_map/all_to_all | solution.py:95
  (6 other events, 41.7 us)
Sparse Core Ops, SparseCore 0:
  10.8 138.2 all-reduce.3
where the time goes:
time: 642 us; the launch traced here: 640 us
  waiting for transfers between devices  425 us (66%)
  starting transfers between devices  119 us (19%)
  other arithmetic  60.1 us (9%)
  local copies, waits for them, and re-layouts  17.1 us (3%)
  between operations  14.9 us (2%)
    ppermute x31, waiting for transfers between devices, from_behind(): lax.ppermute(value, axis, [(source, source + steps) for source in range(l...  283 us
    psum x1, waiting for transfers between devices, per_device(): shear = lax.psum(local_terms, 'depth')  130 us
    ppermute x31, starting transfers between devices, from_behind(): lax.ppermute(value, axis, [(source, source + steps) for source in range(l...  60.4 us
    all_to_all x1, starting transfers between devices, per_device(): lax.all_to_all(send_data.reshape(n_tile, slots, 2, width), 'tile', split_...  43.4 us
    sub x31, other arithmetic, sweep(): new_one = xb_one - (jxx[0] * tp_one + jxy[0] * tp_two)  27.6 us
  transfers between devices with their start and end apart: 38, of which 35 were waited for; matrix products, arithmetic and copies ran while one was open for 11% of the time, Pallas kernels for 0%

commit v1 on v0

--- a/solution.py
+++ b/solution.py
@@ -53,7 +53,11 @@
             -jnp.sum(plane_weight[:, None] * jxy, axis=0),
         ]
     )
-    shear = lax.psum(local_terms, "depth")
+
+    def lift_files(field_in):
+        return jnp.sum(jax.lax.all_gather(field_in, "depth"), axis=0)
+
+    shear = lift_files(local_terms)
     cross = -shear[0] * jnp.sin(2.0 * ray_angle) + shear[1] * jnp.cos(2.0 * ray_angle)
     seed_state = jnp.stack(
         [

time: 642 us -> 580 us (0.903)
  waiting for transfers between devices: 425 us -> 362 us
    psum x1 -> x0, waiting for transfers between devices: 130 us -> none  [per_device(): shear = lax.psum(local_terms, 'depth')]
    all_gather x0 -> x1, waiting for transfers between devices: none -> 67.7 us  [lift_files(): return jnp.sum(jax.lax.all_gather(field_in, 'depth'), axis=0)]
  transfers between devices with their start and end apart: 38 -> 38, of which waited for: 35 -> 35; matrix products, arithmetic and copies ran while one was open for 11% -> 12% of each run, Pallas kernels for 0% -> 0%
where the time goes in v1:
time: 580 us; the launch traced here: 578 us
  waiting for transfers between devices  362 us (62%)
  starting transfers between devices  117 us (20%)
  other arithmetic  61.9 us (11%)
  local copies, waits for them, and re-layouts  17.1 us (3%)
  between operations  14.9 us (3%)
    ppermute x31, waiting for transfers between devices, from_behind(): lax.ppermute(value, axis, [(source, source + steps) for source in range(l...  282 us
    all_gather x1, waiting for transfers between devices, lift_files(): return jnp.sum(jax.lax.all_gather(field_in, 'depth'), axis=0)  67.7 us
    ppermute x31, starting transfers between devices, from_behind(): lax.ppermute(value, axis, [(source, source + steps) for source in range(l...  60.2 us
    all_to_all x1, starting transfers between devices, per_device(): lax.all_to_all(send_data.reshape(n_tile, slots, 2, width), 'tile', split_...  42.5 us
    sub x31, other arithmetic, sweep(): new_one = xb_one - (jxx[0] * tp_one + jxy[0] * tp_two)  27.6 us
    scatter x1, local copies, waits for them, and re-layouts, per_device(): jnp.zeros((n_tile * slots, 2, width), jnp.float32).at[slot].set(contrib[0])  12.5 us
  transfers between devices with their start and end apart: 38, of which 35 were waited for; matrix products, arithmetic and copies ran while one was open for 12% of the time, Pallas kernels for 0%

profile of v1, /device:TPU:103, one launch (start us, length us, event | category | flops | bytes accessed | tf_op | source)
XLA Modules:
  0.0 577.9 jit_solution(6432754596403429686)
XLA Ops:
  19.2 67.7 %all-gather.4.cloned.1.call-done = f32[32,2,16384]{2,1,0:T(2,128)} async-done(((f32[1,2,16384]{2,1,0:T(2,128)}), f32[32,2,16384]{2,1,0:T(2,128)}) %all-gather.4.cloned.1.call-update) | async-done | bytes 4194320 | tf_op jit(solution)/shard_map/all_gather | solution.py:58
  91.3 386.6 %while.10 = (s32[]{:T(128)}, f32[4,16384]{1,0:T(4,128)S(1)}, pred[]{:T(512)}, f32[1,1,16384]{2,1,0:T(1,128)S(1)}, f32[1]{0:T(128)}, /*index=5*/f32[1,1,16384]{2,...) while((s32[]{:T(128)}, f32[4,16384]{1,0:T(4,128)S(1)}, pred[]{:T(512)}, ...), condition=%wide.region_4.5_spmd, body=%wide.region_3.4_spmd.sunk | while | flops 458754 | bytes 3342474 | solution.py:88
  106.4 8.5 %collective-permute-done = f32[4,16384]{1,0:T(4,128)S(1)} collective-permute-done((f32[4,16384]{1,0:T(4,128)S(1)}, f32[4,16384]{1,0:T(4,128)S(1)}, u32[]{:S(2)}, u32[]{:S(2)}) %collective-permute-start) | collective-permute-done | bytes 262176 | tf_op jit(solution)/shard_map/while/body/eval_jaxpr/ppermute | solution.py:13
  118.3 8.5 %collective-permute-done = f32[4,16384]{1,0:T(4,128)S(1)} collective-permute-done((f32[4,16384]{1,0:T(4,128)S(1)}, f32[4,16384]{1,0:T(4,128)S(1)}, u32[]{:S(2)}, u32[]{:S(2)}) %collective-permute-start) | collective-permute-done | bytes 262176 | tf_op jit(solution)/shard_map/while/body/eval_jaxpr/ppermute | solution.py:13
  130.1 8.5 %collective-permute-done = f32[4,16384]{1,0:T(4,128)S(1)} collective-permute-done((f32[4,16384]{1,0:T(4,128)S(1)}, f32[4,16384]{1,0:T(4,128)S(1)}, u32[]{:S(2)}, u32[]{:S(2)}) %collective-permute-start) | collective-permute-done | bytes 262176 | tf_op jit(solution)/shard_map/while/body/eval_jaxpr/ppermute | solution.py:13
  142.0 8.5 %collective-permute-done = f32[4,16384]{1,0:T(4,128)S(1)} collective-permute-done((f32[4,16384]{1,0:T(4,128)S(1)}, f32[4,16384]{1,0:T(4,128)S(1)}, u32[]{:S(2)}, u32[]{:S(2)}) %collective-permute-start) | collective-permute-done | bytes 262176 | tf_op jit(solution)/shard_map/while/body/eval_jaxpr/ppermute | solution.py:13
  153.8 9.1 %collective-permute-done = f32[4,16384]{1,0:T(4,128)S(1)} collective-permute-done((f32[4,16384]{1,0:T(4,128)S(1)}, f32[4,16384]{1,0:T(4,128)S(1)}, u32[]{:S(2)}, u32[]{:S(2)}) %collective-permute-start) | collective-permute-done | bytes 262176 | tf_op jit(solution)/shard_map/while/body/eval_jaxpr/ppermute | solution.py:13
  166.3 10.3 %collective-permute-done = f32[4,16384]{1,0:T(4,128)S(1)} collective-permute-done((f32[4,16384]{1,0:T(4,128)S(1)}, f32[4,16384]{1,0:T(4,128)S(1)}, u32[]{:S(2)}, u32[]{:S(2)}) %collective-permute-start) | collective-permute-done | bytes 262176 | tf_op jit(solution)/shard_map/while/body/eval_jaxpr/ppermute | solution.py:13
  180.0 11.5 %collective-permute-done = f32[4,16384]{1,0:T(4,128)S(1)} collective-permute-done((f32[4,16384]{1,0:T(4,128)S(1)}, f32[4,16384]{1,0:T(4,128)S(1)}, u32[]{:S(2)}, u32[]{:S(2)}) %collective-permute-start) | collective-permute-done | bytes 262176 | tf_op jit(solution)/shard_map/while/body/eval_jaxpr/ppermute | solution.py:13
  194.8 10.6 %collective-permute-done = f32[4,16384]{1,0:T(4,128)S(1)} collective-permute-done((f32[4,16384]{1,0:T(4,128)S(1)}, f32[4,16384]{1,0:T(4,128)S(1)}, u32[]{:S(2)}, u32[]{:S(2)}) %collective-permute-start) | collective-permute-done | bytes 262176 | tf_op jit(solution)/shard_map/while/body/eval_jaxpr/ppermute | solution.py:13
  208.8 9.8 %collective-permute-done = f32[4,16384]{1,0:T(4,128)S(1)} collective-permute-done((f32[4,16384]{1,0:T(4,128)S(1)}, f32[4,16384]{1,0:T(4,128)S(1)}, u32[]{:S(2)}, u32[]{:S(2)}) %collective-permute-start) | collective-permute-done | bytes 262176 | tf_op jit(solution)/shard_map/while/body/eval_jaxpr/ppermute | solution.py:13
  222.0 8.9 %collective-permute-done = f32[4,16384]{1,0:T(4,128)S(1)} collective-permute-done((f32[4,16384]{1,0:T(4,128)S(1)}, f32[4,16384]{1,0:T(4,128)S(1)}, u32[]{:S(2)}, u32[]{:S(2)}) %collective-permute-start) | collective-permute-done | bytes 262176 | tf_op jit(solution)/shard_map/while/body/eval_jaxpr/ppermute | solution.py:13
  234.2 8.5 %collective-permute-done = f32[4,16384]{1,0:T(4,128)S(1)} collective-permute-done((f32[4,16384]{1,0:T(4,128)S(1)}, f32[4,16384]{1,0:T(4,128)S(1)}, u32[]{:S(2)}, u32[]{:S(2)}) %collective-permute-start) | collective-permute-done | bytes 262176 | tf_op jit(solution)/shard_map/while/body/eval_jaxpr/ppermute | solution.py:13
  246.1 8.5 %collective-permute-done = f32[4,16384]{1,0:T(4,128)S(1)} collective-permute-done((f32[4,16384]{1,0:T(4,128)S(1)}, f32[4,16384]{1,0:T(4,128)S(1)}, u32[]{:S(2)}, u32[]{:S(2)}) %collective-permute-start) | collective-permute-done | bytes 262176 | tf_op jit(solution)/shard_map/while/body/eval_jaxpr/ppermute | solution.py:13
  258.0 8.5 %collective-permute-done = f32[4,16384]{1,0:T(4,128)S(1)} collective-permute-done((f32[4,16384]{1,0:T(4,128)S(1)}, f32[4,16384]{1,0:T(4,128)S(1)}, u32[]{:S(2)}, u32[]{:S(2)}) %collective-permute-start) | collective-permute-done | bytes 262176 | tf_op jit(solution)/shard_map/while/body/eval_jaxpr/ppermute | solution.py:13
  281.7 8.5 %collective-permute-done = f32[4,16384]{1,0:T(4,128)S(1)} collective-permute-done((f32[4,16384]{1,0:T(4,128)S(1)}, f32[4,16384]{1,0:T(4,128)S(1)}, u32[]{:S(2)}, u32[]{:S(2)}) %collective-permute-start) | collective-permute-done | bytes 262176 | tf_op jit(solution)/shard_map/while/body/eval_jaxpr/ppermute | solution.py:13
  293.6 8.5 %collective-permute-done = f32[4,16384]{1,0:T(4,128)S(1)} collective-permute-done((f32[4,16384]{1,0:T(4,128)S(1)}, f32[4,16384]{1,0:T(4,128)S(1)}, u32[]{:S(2)}, u32[]{:S(2)}) %collective-permute-start) | collective-permute-done | bytes 262176 | tf_op jit(solution)/shard_map/while/body/eval_jaxpr/ppermute | solution.py:13
  305.4 8.7 %collective-permute-done = f32[4,16384]{1,0:T(4,128)S(1)} collective-permute-done((f32[4,16384]{1,0:T(4,128)S(1)}, f32[4,16384]{1,0:T(4,128)S(1)}, u32[]{:S(2)}, u32[]{:S(2)}) %collective-permute-start) | collective-permute-done | bytes 262176 | tf_op jit(solution)/shard_map/while/body/eval_jaxpr/ppermute | solution.py:13
  317.5 9.9 %collective-permute-done = f32[4,16384]{1,0:T(4,128)S(1)} collective-permute-done((f32[4,16384]{1,0:T(4,128)S(1)}, f32[4,16384]{1,0:T(4,128)S(1)}, u32[]{:S(2)}, u32[]{:S(2)}) %collective-permute-start) | collective-permute-done | bytes 262176 | tf_op jit(solution)/shard_map/while/body/eval_jaxpr/ppermute | solution.py:13
  330.7 11.0 %collective-permute-done = f32[4,16384]{1,0:T(4,128)S(1)} collective-permute-done((f32[4,16384]{1,0:T(4,128)S(1)}, f32[4,16384]{1,0:T(4,128)S(1)}, u32[]{:S(2)}, u32[]{:S(2)}) %collective-permute-start) | collective-permute-done | bytes 262176 | tf_op jit(solution)/shard_map/while/body/eval_jaxpr/ppermute | solution.py:13
  345.1 10.8 %collective-permute-done = f32[4,16384]{1,0:T(4,128)S(1)} collective-permute-done((f32[4,16384]{1,0:T(4,128)S(1)}, f32[4,16384]{1,0:T(4,128)S(1)}, u32[]{:S(2)}, u32[]{:S(2)}) %collective-permute-start) | collective-permute-done | bytes 262176 | tf_op jit(solution)/shard_map/while/body/eval_jaxpr/ppermute | solution.py:13
  359.2 9.9 %collective-permute-done = f32[4,16384]{1,0:T(4,128)S(1)} collective-permute-done((f32[4,16384]{1,0:T(4,128)S(1)}, f32[4,16384]{1,0:T(4,128)S(1)}, u32[]{:S(2)}, u32[]{:S(2)}) %collective-permute-start) | collective-permute-done | bytes 262176 | tf_op jit(solution)/shard_map/while/body/eval_jaxpr/ppermute | solution.py:13
  372.5 9.0 %collective-permute-done = f32[4,16384]{1,0:T(4,128)S(1)} collective-permute-done((f32[4,16384]{1,0:T(4,128)S(1)}, f32[4,16384]{1,0:T(4,128)S(1)}, u32[]{:S(2)}, u32[]{:S(2)}) %collective-permute-start) | collective-permute-done | bytes 262176 | tf_op jit(solution)/shard_map/while/body/eval_jaxpr/ppermute | solution.py:13
  396.7 8.5 %collective-permute-done = f32[4,16384]{1,0:T(4,128)S(1)} collective-permute-done((f32[4,16384]{1,0:T(4,128)S(1)}, f32[4,16384]{1,0:T(4,128)S(1)}, u32[]{:S(2)}, u32[]{:S(2)}) %collective-permute-start) | collective-permute-done | bytes 262176 | tf_op jit(solution)/shard_map/while/body/eval_jaxpr/ppermute | solution.py:13
  408.6 8.5 %collective-permute-done = f32[4,16384]{1,0:T(4,128)S(1)} collective-permute-done((f32[4,16384]{1,0:T(4,128)S(1)}, f32[4,16384]{1,0:T(4,128)S(1)}, u32[]{:S(2)}, u32[]{:S(2)}) %collective-permute-start) | collective-permute-done | bytes 262176 | tf_op jit(solution)/shard_map/while/body/eval_jaxpr/ppermute | solution.py:13
  420.5 8.5 %collective-permute-done = f32[4,16384]{1,0:T(4,128)S(1)} collective-permute-done((f32[4,16384]{1,0:T(4,128)S(1)}, f32[4,16384]{1,0:T(4,128)S(1)}, u32[]{:S(2)}, u32[]{:S(2)}) %collective-permute-start) | collective-permute-done | bytes 262176 | tf_op jit(solution)/shard_map/while/body/eval_jaxpr/ppermute | solution.py:13
  432.3 8.5 %collective-permute-done = f32[4,16384]{1,0:T(4,128)S(1)} collective-permute-done((f32[4,16384]{1,0:T(4,128)S(1)}, f32[4,16384]{1,0:T(4,128)S(1)}, u32[]{:S(2)}, u32[]{:S(2)}) %collective-permute-start) | collective-permute-done | bytes 262176 | tf_op jit(solution)/shard_map/while/body/eval_jaxpr/ppermute | solution.py:13
  456.1 8.6 %collective-permute-done = f32[4,16384]{1,0:T(4,128)S(1)} collective-permute-done((f32[4,16384]{1,0:T(4,128)S(1)}, f32[4,16384]{1,0:T(4,128)S(1)}, u32[]{:S(2)}, u32[]{:S(2)}) %collective-permute-start) | collective-permute-done | bytes 262176 | tf_op jit(solution)/shard_map/while/body/eval_jaxpr/ppermute | solution.py:13
  468.0 9.8 %collective-permute-done = f32[4,16384]{1,0:T(4,128)S(1)} collective-permute-done((f32[4,16384]{1,0:T(4,128)S(1)}, f32[4,16384]{1,0:T(4,128)S(1)}, u32[]{:S(2)}, u32[]{:S(2)}) %collective-permute-start) | collective-permute-done | bytes 262176 | tf_op jit(solution)/shard_map/while/body/eval_jaxpr/ppermute | solution.py:13
  482.3 12.5 %scatter_fusion = f32[256,2,128]{2,1,0:T(2,128)} fusion(f32[256,2,128]{2,1,0:T(2,128)} %broadcast.154.clone, s32[128]{0:T(128)S(1)} %fusion.14, f32[128,2,128]{2,1,0:T(2,128)S(1)} %fusion.4), kind=kCustom, calls=%fused_computation.1 | custom fusion | bytes 393728 | tf_op jit(solution)/shard_map/scatter | solution.py:97
  494.8 42.5 %all-to-all-start.1 = ((f32[8,32,2,128]{3,2,1,0:T(2,128)}), f32[8,32,2,128]{3,2,1,0:T(2,128)S(1)}, u32[]{:S(2)}, u32[]{:S(2)}) async-start(f32[8,32,2,128]{3,2,1,0:T(2,128)} %bitcast.22), calls=%async_computation.1 | async-start | bytes 524288 | tf_op jit(solution)/shard_map/all_to_all | solution.py:99
  543.8 8.7 %scatter_fusion.1 = f32[256,2,128]{2,1,0:T(2,128)S(1)} fusion(f32[256,2,128]{2,1,0:T(2,128)S(1)} %broadcast.154, s32[256]{0:T(256)S(1)} %bitcast.87, f32[256,2,128]{2,1,0:T(2,128)S(1)} %bitcast.82), kind=kCustom, calls=%fused_computation.2 | custom fusion | flops 65536 | bytes 787456 | tf_op jit(solution)/shard_map/scatter-add | solution.py:108
  (204 shorter events, 181.6 us)
Async XLA Ops:
  6.5 80.4 %all-gather.4.cloned.1.call-start = ((), (), s32[]{:S(2)}) async-start(), calls=%async_computation.2 | async-start | bytes 4325376 | tf_op jit(solution)/shard_map/all_gather | solution.py:58
  12.4 482.3 %all-to-all-start = ((s32[8,1,32]{2,1,0:T(1,128)}), s32[8,1,32]{2,1,0:T(1,128)S(1)}, u32[]{:S(2)}, u32[]{:S(2)}) async-start(s32[8,1,32]{2,1,0:T(1,128)} %all_to_all.9), calls=%async_computation | async-start | bytes 8192 | tf_op jit(solution)/shard_map/all_to_all | solution.py:102
  92.6 10.4 %collective-permute-start = (f32[4,16384]{1,0:T(4,128)S(1)}, f32[4,16384]{1,0:T(4,128)S(1)}, u32[]{:S(2)}, u32[]{:S(2)}) collective-permute-start(f32[4,16384]{1,0:T(4,128)S(1)} %pad_maximum_fusion.6), channel_id=1, source_target_pairs={{8,0},{16,8},{24,16},{32,24},{40,32},{48,40},{56,48},{64,56},{72,6... | collective-permute-start | bytes 786440 | tf_op jit(solution)/shard_map/while/body/eval_jaxpr/ppermute | solution.py:13
  104.5 10.4 %collective-permute-start = (f32[4,16384]{1,0:T(4,128)S(1)}, f32[4,16384]{1,0:T(4,128)S(1)}, u32[]{:S(2)}, u32[]{:S(2)}) collective-permute-start(f32[4,16384]{1,0:T(4,128)S(1)} %pad_maximum_fusion.6), channel_id=1, source_target_pairs={{8,0},{16,8},{24,16},{32,24},{40,32},{48,40},{56,48},{64,56},{72,6... | collective-permute-start | bytes 786440 | tf_op jit(solution)/shard_map/while/body/eval_jaxpr/ppermute | solution.py:13
  116.3 10.4 %collective-permute-start = (f32[4,16384]{1,0:T(4,128)S(1)}, f32[4,16384]{1,0:T(4,128)S(1)}, u32[]{:S(2)}, u32[]{:S(2)}) collective-permute-start(f32[4,16384]{1,0:T(4,128)S(1)} %pad_maximum_fusion.6), channel_id=1, source_target_pairs={{8,0},{16,8},{24,16},{32,24},{40,32},{48,40},{56,48},{64,56},{72,6... | collective-permute-start | bytes 786440 | tf_op jit(solution)/shard_map/while/body/eval_jaxpr/ppermute | solution.py:13
  128.2 10.4 %collective-permute-start = (f32[4,16384]{1,0:T(4,128)S(1)}, f32[4,16384]{1,0:T(4,128)S(1)}, u32[]{:S(2)}, u32[]{:S(2)}) collective-permute-start(f32[4,16384]{1,0:T(4,128)S(1)} %pad_maximum_fusion.6), channel_id=1, source_target_pairs={{8,0},{16,8},{24,16},{32,24},{40,32},{48,40},{56,48},{64,56},{72,6... | collective-permute-start | bytes 786440 | tf_op jit(solution)/shard_map/while/body/eval_jaxpr/ppermute | solution.py:13
  140.1 10.4 %collective-permute-start = (f32[4,16384]{1,0:T(4,128)S(1)}, f32[4,16384]{1,0:T(4,128)S(1)}, u32[]{:S(2)}, u32[]{:S(2)}) collective-permute-start(f32[4,16384]{1,0:T(4,128)S(1)} %pad_maximum_fusion.6), channel_id=1, source_target_pairs={{8,0},{16,8},{24,16},{32,24},{40,32},{48,40},{56,48},{64,56},{72,6... | collective-permute-start | bytes 786440 | tf_op jit(solution)/shard_map/while/body/eval_jaxpr/ppermute | solution.py:13
  151.9 11.1 %collective-permute-start = (f32[4,16384]{1,0:T(4,128)S(1)}, f32[4,16384]{1,0:T(4,128)S(1)}, u32[]{:S(2)}, u32[]{:S(2)}) collective-permute-start(f32[4,16384]{1,0:T(4,128)S(1)} %pad_maximum_fusion.6), channel_id=1, source_target_pairs={{8,0},{16,8},{24,16},{32,24},{40,32},{48,40},{56,48},{64,56},{72,6... | collective-permute-start | bytes 786440 | tf_op jit(solution)/shard_map/while/body/eval_jaxpr/ppermute | solution.py:13
  164.4 12.2 %collective-permute-start = (f32[4,16384]{1,0:T(4,128)S(1)}, f32[4,16384]{1,0:T(4,128)S(1)}, u32[]{:S(2)}, u32[]{:S(2)}) collective-permute-start(f32[4,16384]{1,0:T(4,128)S(1)} %pad_maximum_fusion.6), channel_id=1, source_target_pairs={{8,0},{16,8},{24,16},{32,24},{40,32},{48,40},{56,48},{64,56},{72,6... | collective-permute-start | bytes 786440 | tf_op jit(solution)/shard_map/while/body/eval_jaxpr/ppermute | solution.py:13
  178.0 13.4 %collective-permute-start = (f32[4,16384]{1,0:T(4,128)S(1)}, f32[4,16384]{1,0:T(4,128)S(1)}, u32[]{:S(2)}, u32[]{:S(2)}) collective-permute-start(f32[4,16384]{1,0:T(4,128)S(1)} %pad_maximum_fusion.6), channel_id=1, source_target_pairs={{8,0},{16,8},{24,16},{32,24},{40,32},{48,40},{56,48},{64,56},{72,6... | collective-permute-start | bytes 786440 | tf_op jit(solution)/shard_map/while/body/eval_jaxpr/ppermute | solution.py:13
  192.9 12.6 %collective-permute-start = (f32[4,16384]{1,0:T(4,128)S(1)}, f32[4,16384]{1,0:T(4,128)S(1)}, u32[]{:S(2)}, u32[]{:S(2)}) collective-permute-start(f32[4,16384]{1,0:T(4,128)S(1)} %pad_maximum_fusion.6), channel_id=1, source_target_pairs={{8,0},{16,8},{24,16},{32,24},{40,32},{48,40},{56,48},{64,56},{72,6... | collective-permute-start | bytes 786440 | tf_op jit(solution)/shard_map/while/body/eval_jaxpr/ppermute | solution.py:13
  206.9 11.7 %collective-permute-start = (f32[4,16384]{1,0:T(4,128)S(1)}, f32[4,16384]{1,0:T(4,128)S(1)}, u32[]{:S(2)}, u32[]{:S(2)}) collective-permute-start(f32[4,16384]{1,0:T(4,128)S(1)} %pad_maximum_fusion.6), channel_id=1, source_target_pairs={{8,0},{16,8},{24,16},{32,24},{40,32},{48,40},{56,48},{64,56},{72,6... | collective-permute-start | bytes 786440 | tf_op jit(solution)/shard_map/while/body/eval_jaxpr/ppermute | solution.py:13
  220.0 10.9 %collective-permute-start = (f32[4,16384]{1,0:T(4,128)S(1)}, f32[4,16384]{1,0:T(4,128)S(1)}, u32[]{:S(2)}, u32[]{:S(2)}) collective-permute-start(f32[4,16384]{1,0:T(4,128)S(1)} %pad_maximum_fusion.6), channel_id=1, source_target_pairs={{8,0},{16,8},{24,16},{32,24},{40,32},{48,40},{56,48},{64,56},{72,6... | collective-permute-start | bytes 786440 | tf_op jit(solution)/shard_map/while/body/eval_jaxpr/ppermute | solution.py:13
  232.3 10.4 %collective-permute-start = (f32[4,16384]{1,0:T(4,128)S(1)}, f32[4,16384]{1,0:T(4,128)S(1)}, u32[]{:S(2)}, u32[]{:S(2)}) collective-permute-start(f32[4,16384]{1,0:T(4,128)S(1)} %pad_maximum_fusion.6), channel_id=1, source_target_pairs={{8,0},{16,8},{24,16},{32,24},{40,32},{48,40},{56,48},{64,56},{72,6... | collective-permute-start | bytes 786440 | tf_op jit(solution)/shard_map/while/body/eval_jaxpr/ppermute | solution.py:13
  244.2 10.4 %collective-permute-start = (f32[4,16384]{1,0:T(4,128)S(1)}, f32[4,16384]{1,0:T(4,128)S(1)}, u32[]{:S(2)}, u32[]{:S(2)}) collective-permute-start(f32[4,16384]{1,0:T(4,128)S(1)} %pad_maximum_fusion.6), channel_id=1, source_target_pairs={{8,0},{16,8},{24,16},{32,24},{40,32},{48,40},{56,48},{64,56},{72,6... | collective-permute-start | bytes 786440 | tf_op jit(solution)/shard_map/while/body/eval_jaxpr/ppermute | solution.py:13
  256.0 10.4 %collective-permute-start = (f32[4,16384]{1,0:T(4,128)S(1)}, f32[4,16384]{1,0:T(4,128)S(1)}, u32[]{:S(2)}, u32[]{:S(2)}) collective-permute-start(f32[4,16384]{1,0:T(4,128)S(1)} %pad_maximum_fusion.6), channel_id=1, source_target_pairs={{8,0},{16,8},{24,16},{32,24},{40,32},{48,40},{56,48},{64,56},{72,6... | collective-permute-start | bytes 786440 | tf_op jit(solution)/shard_map/while/body/eval_jaxpr/ppermute | solution.py:13
  267.9 10.4 %collective-permute-start = (f32[4,16384]{1,0:T(4,128)S(1)}, f32[4,16384]{1,0:T(4,128)S(1)}, u32[]{:S(2)}, u32[]{:S(2)}) collective-permute-start(f32[4,16384]{1,0:T(4,128)S(1)} %pad_maximum_fusion.6), channel_id=1, source_target_pairs={{8,0},{16,8},{24,16},{32,24},{40,32},{48,40},{56,48},{64,56},{72,6... | collective-permute-start | bytes 786440 | tf_op jit(solution)/shard_map/while/body/eval_jaxpr/ppermute | solution.py:13
  279.8 10.4 %collective-permute-start = (f32[4,16384]{1,0:T(4,128)S(1)}, f32[4,16384]{1,0:T(4,128)S(1)}, u32[]{:S(2)}, u32[]{:S(2)}) collective-permute-start(f32[4,16384]{1,0:T(4,128)S(1)} %pad_maximum_fusion.6), channel_id=1, source_target_pairs={{8,0},{16,8},{24,16},{32,24},{40,32},{48,40},{56,48},{64,56},{72,6... | collective-permute-start | bytes 786440 | tf_op jit(solution)/shard_map/while/body/eval_jaxpr/ppermute | solution.py:13
  291.6 10.4 %collective-permute-start = (f32[4,16384]{1,0:T(4,128)S(1)}, f32[4,16384]{1,0:T(4,128)S(1)}, u32[]{:S(2)}, u32[]{:S(2)}) collective-permute-start(f32[4,16384]{1,0:T(4,128)S(1)} %pad_maximum_fusion.6), channel_id=1, source_target_pairs={{8,0},{16,8},{24,16},{32,24},{40,32},{48,40},{56,48},{64,56},{72,6... | collective-permute-start | bytes 786440 | tf_op jit(solution)/shard_map/while/body/eval_jaxpr/ppermute | solution.py:13
  303.5 10.7 %collective-permute-start = (f32[4,16384]{1,0:T(4,128)S(1)}, f32[4,16384]{1,0:T(4,128)S(1)}, u32[]{:S(2)}, u32[]{:S(2)}) collective-permute-start(f32[4,16384]{1,0:T(4,128)S(1)} %pad_maximum_fusion.6), channel_id=1, source_target_pairs={{8,0},{16,8},{24,16},{32,24},{40,32},{48,40},{56,48},{64,56},{72,6... | collective-permute-start | bytes 786440 | tf_op jit(solution)/shard_map/while/body/eval_jaxpr/ppermute | solution.py:13
  315.6 11.8 %collective-permute-start = (f32[4,16384]{1,0:T(4,128)S(1)}, f32[4,16384]{1,0:T(4,128)S(1)}, u32[]{:S(2)}, u32[]{:S(2)}) collective-permute-start(f32[4,16384]{1,0:T(4,128)S(1)} %pad_maximum_fusion.6), channel_id=1, source_target_pairs={{8,0},{16,8},{24,16},{32,24},{40,32},{48,40},{56,48},{64,56},{72,6... | collective-permute-start | bytes 786440 | tf_op jit(solution)/shard_map/while/body/eval_jaxpr/ppermute | solution.py:13
  328.8 13.0 %collective-permute-start = (f32[4,16384]{1,0:T(4,128)S(1)}, f32[4,16384]{1,0:T(4,128)S(1)}, u32[]{:S(2)}, u32[]{:S(2)}) collective-permute-start(f32[4,16384]{1,0:T(4,128)S(1)} %pad_maximum_fusion.6), channel_id=1, source_target_pairs={{8,0},{16,8},{24,16},{32,24},{40,32},{48,40},{56,48},{64,56},{72,6... | collective-permute-start | bytes 786440 | tf_op jit(solution)/shard_map/while/body/eval_jaxpr/ppermute | solution.py:13
  343.2 12.7 %collective-permute-start = (f32[4,16384]{1,0:T(4,128)S(1)}, f32[4,16384]{1,0:T(4,128)S(1)}, u32[]{:S(2)}, u32[]{:S(2)}) collective-permute-start(f32[4,16384]{1,0:T(4,128)S(1)} %pad_maximum_fusion.6), channel_id=1, source_target_pairs={{8,0},{16,8},{24,16},{32,24},{40,32},{48,40},{56,48},{64,56},{72,6... | collective-permute-start | bytes 786440 | tf_op jit(solution)/shard_map/while/body/eval_jaxpr/ppermute | solution.py:13
  357.3 11.8 %collective-permute-start = (f32[4,16384]{1,0:T(4,128)S(1)}, f32[4,16384]{1,0:T(4,128)S(1)}, u32[]{:S(2)}, u32[]{:S(2)}) collective-permute-start(f32[4,16384]{1,0:T(4,128)S(1)} %pad_maximum_fusion.6), channel_id=1, source_target_pairs={{8,0},{16,8},{24,16},{32,24},{40,32},{48,40},{56,48},{64,56},{72,6... | collective-permute-start | bytes 786440 | tf_op jit(solution)/shard_map/while/body/eval_jaxpr/ppermute | solution.py:13
  370.6 11.0 %collective-permute-start = (f32[4,16384]{1,0:T(4,128)S(1)}, f32[4,16384]{1,0:T(4,128)S(1)}, u32[]{:S(2)}, u32[]{:S(2)}) collective-permute-start(f32[4,16384]{1,0:T(4,128)S(1)} %pad_maximum_fusion.6), channel_id=1, source_target_pairs={{8,0},{16,8},{24,16},{32,24},{40,32},{48,40},{56,48},{64,56},{72,6... | collective-permute-start | bytes 786440 | tf_op jit(solution)/shard_map/while/body/eval_jaxpr/ppermute | solution.py:13
  394.8 10.4 %collective-permute-start = (f32[4,16384]{1,0:T(4,128)S(1)}, f32[4,16384]{1,0:T(4,128)S(1)}, u32[]{:S(2)}, u32[]{:S(2)}) collective-permute-start(f32[4,16384]{1,0:T(4,128)S(1)} %pad_maximum_fusion.6), channel_id=1, source_target_pairs={{8,0},{16,8},{24,16},{32,24},{40,32},{48,40},{56,48},{64,56},{72,6... | collective-permute-start | bytes 786440 | tf_op jit(solution)/shard_map/while/body/eval_jaxpr/ppermute | solution.py:13
  406.7 10.4 %collective-permute-start = (f32[4,16384]{1,0:T(4,128)S(1)}, f32[4,16384]{1,0:T(4,128)S(1)}, u32[]{:S(2)}, u32[]{:S(2)}) collective-permute-start(f32[4,16384]{1,0:T(4,128)S(1)} %pad_maximum_fusion.6), channel_id=1, source_target_pairs={{8,0},{16,8},{24,16},{32,24},{40,32},{48,40},{56,48},{64,56},{72,6... | collective-permute-start | bytes 786440 | tf_op jit(solution)/shard_map/while/body/eval_jaxpr/ppermute | solution.py:13
  418.5 10.4 %collective-permute-start = (f32[4,16384]{1,0:T(4,128)S(1)}, f32[4,16384]{1,0:T(4,128)S(1)}, u32[]{:S(2)}, u32[]{:S(2)}) collective-permute-start(f32[4,16384]{1,0:T(4,128)S(1)} %pad_maximum_fusion.6), channel_id=1, source_target_pairs={{8,0},{16,8},{24,16},{32,24},{40,32},{48,40},{56,48},{64,56},{72,6... | collective-permute-start | bytes 786440 | tf_op jit(solution)/shard_map/while/body/eval_jaxpr/ppermute | solution.py:13
  430.4 10.4 %collective-permute-start = (f32[4,16384]{1,0:T(4,128)S(1)}, f32[4,16384]{1,0:T(4,128)S(1)}, u32[]{:S(2)}, u32[]{:S(2)}) collective-permute-start(f32[4,16384]{1,0:T(4,128)S(1)} %pad_maximum_fusion.6), channel_id=1, source_target_pairs={{8,0},{16,8},{24,16},{32,24},{40,32},{48,40},{56,48},{64,56},{72,6... | collective-permute-start | bytes 786440 | tf_op jit(solution)/shard_map/while/body/eval_jaxpr/ppermute | solution.py:13
  454.1 10.6 %collective-permute-start = (f32[4,16384]{1,0:T(4,128)S(1)}, f32[4,16384]{1,0:T(4,128)S(1)}, u32[]{:S(2)}, u32[]{:S(2)}) collective-permute-start(f32[4,16384]{1,0:T(4,128)S(1)} %pad_maximum_fusion.6), channel_id=1, source_target_pairs={{8,0},{16,8},{24,16},{32,24},{40,32},{48,40},{56,48},{64,56},{72,6... | collective-permute-start | bytes 786440 | tf_op jit(solution)/shard_map/while/body/eval_jaxpr/ppermute | solution.py:13
  466.1 11.7 %collective-permute-start = (f32[4,16384]{1,0:T(4,128)S(1)}, f32[4,16384]{1,0:T(4,128)S(1)}, u32[]{:S(2)}, u32[]{:S(2)}) collective-permute-start(f32[4,16384]{1,0:T(4,128)S(1)} %pad_maximum_fusion.6), channel_id=1, source_target_pairs={{8,0},{16,8},{24,16},{32,24},{40,32},{48,40},{56,48},{64,56},{72,6... | collective-permute-start | bytes 786440 | tf_op jit(solution)/shard_map/while/body/eval_jaxpr/ppermute | solution.py:13
  494.8 49.0 %all-to-all-start.1 = ((f32[8,32,2,128]{3,2,1,0:T(2,128)}), f32[8,32,2,128]{3,2,1,0:T(2,128)S(1)}, u32[]{:S(2)}, u32[]{:S(2)}) async-start(f32[8,32,2,128]{3,2,1,0:T(2,128)} %bitcast.22), calls=%async_computation.1 | async-start | bytes 524288 | tf_op jit(solution)/shard_map/all_to_all | solution.py:99
  (7 other events, 125.7 us)
Sparse Core Ops, SparseCore 0:
  9.9 76.9 all-gather.3
